TPU v7x, 32 devices: a whole 2x2x4 slice. The times are simulated.
32 devices in a mesh: site: 4 (over y, x), bond: 8 (over z, core).
Axes of the slice: x: 2, y: 2, z: 4, core: 2. Of those that a mesh axis runs over, the one named last changes fastest.
Arguments:
- start_rows: bfloat16 [1024, 4096], P(None, 'bond'), may hold values from -6 to 6
- site_tensors: bfloat16 [4, 4096, 8, 4096], P('site', None, None, 'bond'), may hold values from -0.09375 to 0.09375
- block_scales: float32 [4, 8, 32], P('site', None, 'bond'), may hold values from 0.25 to 1
- displacement: float32 [4, 8, 8], P('site'), may hold values from -0.9 to 0.9
- outcomes: int32 [4, 1024], P('site'), may hold values from 0 to 7
Outputs:
- leaving: bfloat16 [4, 1024, 4096], P('site', None, 'bond')
- log_norms: float32 [4, 1024], P('site')
Inputs may be any that keep to these rules, and one draw needn't show every extreme that they name: outcomes index the second dimension of displacement.
All inputs are finite; a program needn't handle non-finite values.
Results may differ from a plain program's by a relative error of at most 0.014.
Values may be sent and summed in bfloat16 or wider, within the bound.
A program may use at most 128 MiB of HBM per device.

v0:
```python
import jax
import jax.numpy as jnp
from jax import lax
from jax.sharding import PartitionSpec as P

ROWS = 512


def shifted(value, axis, steps):
    count = lax.axis_size(axis)
    initial, last = (max(0, -steps), min(count, count - steps))
    return lax.ppermute(value, axis, [(source, source + steps) for source in range(initial, last)])


def local(start_rows, site_tensors, block_scales, displacement, outcomes):
    sites = lax.axis_size("site")
    cols = site_tensors.shape[3]
    chi = site_tensors.shape[1]
    phys = site_tensors.shape[2]
    nblk = block_scales.shape[2]
    allrows = start_rows.shape[0]
    grows = ROWS
    ngroups = allrows // grows
    ticks = ngroups + sites - 1
    a_mat = site_tensors[0].reshape(chi, phys * cols)
    scales = block_scales[0][:, :, None]
    table = displacement[0]
    outcome_row = outcomes[0]
    position = lax.axis_index("site")

    def tick(step, carry):
        incoming, incoming_norm, out_leave, out_logs = carry
        batch = step - position
        valid = jnp.logical_and(batch >= 0, batch < ngroups)
        first = jnp.clip(batch, 0, ngroups - 1) * grows
        start_piece = lax.dynamic_slice_in_dim(start_rows, first, grows, 0)
        rows_in = jnp.where(position == 0, start_piece, incoming)
        piece = lax.all_gather(rows_in, "bond", axis=1, tiled=True)
        total = jnp.dot(piece, a_mat, preferred_element_type=jnp.float32)
        pf = piece.astype(jnp.float32)
        total, squares = (total, jnp.sum(pf * pf, axis=1))
        local_norm = jnp.sqrt(squares / chi + 1e-06)
        prod = total.reshape(grows, phys, nblk, cols // nblk) * scales[None]
        prod = prod.reshape(grows, phys, cols)
        picked = lax.dynamic_slice_in_dim(outcome_row, first, grows, 0)
        onehot = (picked[:, None] == jnp.arange(phys, dtype=jnp.int32)[None, :]).astype(jnp.float32)
        weight = jnp.dot(onehot, table, precision=lax.Precision.HIGHEST)
        mixed = jnp.sum(weight[:, :, None] * prod, axis=1)
        leave = (mixed / local_norm[:, None]).astype(jnp.bfloat16)
        out_leave = jnp.where(
            valid, lax.dynamic_update_slice_in_dim(out_leave, leave, first, 0), out_leave
        )
        out_logs = jnp.where(
            valid,
            lax.dynamic_update_slice_in_dim(out_logs, jnp.log(local_norm), first, 0),
            out_logs,
        )
        incoming = shifted(leave, "site", 1)
        return (incoming, incoming_norm, out_leave, out_logs)

    carry = (
        jnp.zeros((grows, cols), jnp.bfloat16),
        jnp.ones((grows,), jnp.float32),
        jnp.zeros((allrows, cols), jnp.bfloat16),
        jnp.zeros((allrows,), jnp.float32),
    )
    carry = lax.fori_loop(0, ticks, tick, carry)
    return (carry[2][None], carry[3][None])


def solution(mesh):
    return jax.shard_map(
        local,
        mesh=mesh,
        in_specs=(
            P(None, "bond"),
            P("site", None, None, "bond"),
            P("site", None, "bond"),
            P("site", None, None),
            P("site", None),
        ),
        out_specs=(P("site", None, "bond"), P("site", None)),
        check_vma=False,
    )
```

profile of v0, /device:TPU:4, one launch (start us, length us, event | category | flops | bytes accessed | tf_op | source)
XLA Modules:
  0.0 550.5 jit_solution(6089565585654436752)
XLA Ops:
  7.2 22.7 %copy.10 = bf16[512,8,8,512]{3,1,2,0:T(8,128)(2,1)} copy(bf16[512,8,8,512]{3,2,1,0:T(8,128)(2,1)} %bitcast.35) | data formatting | bytes 67108864
  31.1 512.3 %while.18 = (s32[]{:T(128)}, bf16[512,512]{1,0:T(8,128)(2,1)S(1)}, bf16[1024,512]{1,0:T(8,128)(2,1)}, f32[1024]{0:T(1024)S(1)}, s32[]{:T(128)}, /*index=5*/s32[1...) while((s32[]{:T(128)}, bf16[512,512]{1,0:T(8,128)(2,1)S(1)}, ...), condition=%wide.region_3.4_spmd, body=%wide.region_0.3_spmd.sunk | while | flops 17193637888 | bytes 113855224 | solution.py:67
  33.6 47.9 %all-gather.2.cloned.1.call-done = bf16[512,4096]{1,0:T(8,128)(2,1)} async-done(((bf16[512,512]{1,0:T(8,128)(2,1)}), bf16[512,4096]{1,0:T(8,128)(2,1)}) %all-gather.2.cloned.1.call-update) | async-done | bytes 4194320 | tf_op jit(solution)/shard_map/while/body/eval_jaxpr/all_gather | solution.py:38
  81.6 22.6 %fusion.18 = f32[512,4096]{1,0:T(8,128)S(1)} fusion(bf16[512,4096]{1,0:T(8,128)(2,1)} %all-gather.2.cloned.1.call-done, bf16[4096,4096]{1,0:T(8,128)(2,1)} %get-tuple-element.361), kind=kOutput, calls=%fused_computation.14.clone.1 | convolution fusion | flops 17179869184 | bytes 46137344 | tf_op jit(solution)/shard_map/while/body/eval_jaxpr/dot_general | solution.py:39
  104.2 8.2 %copy.12 = f32[64,8,8,512]{3,2,1,0:T(8,128)S(1)} copy(f32[64,8,8,512]{3,1,2,0:T(8,128)S(1)} %bitcast.34) | data formatting | bytes 16777216 | tf_op jit(solution)/shard_map/while
  113.5 3.9 fusion.20
  119.4 3.4 collective-permute-start
  122.8 13.5 %collective-permute-done = bf16[512,512]{1,0:T(8,128)(2,1)S(1)} collective-permute-done((bf16[512,512]{1,0:T(8,128)(2,1)S(1)}, bf16[512,512]{1,0:T(8,128)(2,1)S(1)}, u32[]{:S(2)}, u32[]{:S(2)}) %collective-permute-start) | collective-permute-done | bytes 524320 | tf_op jit(solution)/shard_map/while/body/eval_jaxpr/ppermute | solution.py:12
  138.8 44.7 %all-gather.2.cloned.1.call-done = bf16[512,4096]{1,0:T(8,128)(2,1)} async-done(((bf16[512,512]{1,0:T(8,128)(2,1)}), bf16[512,4096]{1,0:T(8,128)(2,1)}) %all-gather.2.cloned.1.call-update) | async-done | bytes 4194320 | tf_op jit(solution)/shard_map/while/body/eval_jaxpr/all_gather | solution.py:38
  183.5 22.6 %fusion.18 = f32[512,4096]{1,0:T(8,128)S(1)} fusion(bf16[512,4096]{1,0:T(8,128)(2,1)} %all-gather.2.cloned.1.call-done, bf16[4096,4096]{1,0:T(8,128)(2,1)} %get-tuple-element.361), kind=kOutput, calls=%fused_computation.14.clone.1 | convolution fusion | flops 17179869184 | bytes 46137344 | tf_op jit(solution)/shard_map/while/body/eval_jaxpr/dot_general | solution.py:39
  206.1 8.2 %copy.12 = f32[64,8,8,512]{3,2,1,0:T(8,128)S(1)} copy(f32[64,8,8,512]{3,1,2,0:T(8,128)S(1)} %bitcast.34) | data formatting | bytes 16777216 | tf_op jit(solution)/shard_map/while
  215.4 3.9 fusion.20
  221.4 3.4 collective-permute-start
  224.7 13.5 %collective-permute-done = bf16[512,512]{1,0:T(8,128)(2,1)S(1)} collective-permute-done((bf16[512,512]{1,0:T(8,128)(2,1)S(1)}, bf16[512,512]{1,0:T(8,128)(2,1)S(1)}, u32[]{:S(2)}, u32[]{:S(2)}) %collective-permute-start) | collective-permute-done | bytes 524320 | tf_op jit(solution)/shard_map/while/body/eval_jaxpr/ppermute | solution.py:12
  240.7 44.7 %all-gather.2.cloned.1.call-done = bf16[512,4096]{1,0:T(8,128)(2,1)} async-done(((bf16[512,512]{1,0:T(8,128)(2,1)}), bf16[512,4096]{1,0:T(8,128)(2,1)}) %all-gather.2.cloned.1.call-update) | async-done | bytes 4194320 | tf_op jit(solution)/shard_map/while/body/eval_jaxpr/all_gather | solution.py:38
  285.4 22.6 %fusion.18 = f32[512,4096]{1,0:T(8,128)S(1)} fusion(bf16[512,4096]{1,0:T(8,128)(2,1)} %all-gather.2.cloned.1.call-done, bf16[4096,4096]{1,0:T(8,128)(2,1)} %get-tuple-element.361), kind=kOutput, calls=%fused_computation.14.clone.1 | convolution fusion | flops 17179869184 | bytes 46137344 | tf_op jit(solution)/shard_map/while/body/eval_jaxpr/dot_general | solution.py:39
  308.0 8.2 %copy.12 = f32[64,8,8,512]{3,2,1,0:T(8,128)S(1)} copy(f32[64,8,8,512]{3,1,2,0:T(8,128)S(1)} %bitcast.34) | data formatting | bytes 16777216 | tf_op jit(solution)/shard_map/while
  317.3 3.9 fusion.20
  323.3 3.4 collective-permute-start
  326.6 13.5 %collective-permute-done = bf16[512,512]{1,0:T(8,128)(2,1)S(1)} collective-permute-done((bf16[512,512]{1,0:T(8,128)(2,1)S(1)}, bf16[512,512]{1,0:T(8,128)(2,1)S(1)}, u32[]{:S(2)}, u32[]{:S(2)}) %collective-permute-start) | collective-permute-done | bytes 524320 | tf_op jit(solution)/shard_map/while/body/eval_jaxpr/ppermute | solution.py:12
  342.6 44.4 %all-gather.2.cloned.1.call-done = bf16[512,4096]{1,0:T(8,128)(2,1)} async-done(((bf16[512,512]{1,0:T(8,128)(2,1)}), bf16[512,4096]{1,0:T(8,128)(2,1)}) %all-gather.2.cloned.1.call-update) | async-done | bytes 4194320 | tf_op jit(solution)/shard_map/while/body/eval_jaxpr/all_gather | solution.py:38
  387.0 22.6 %fusion.18 = f32[512,4096]{1,0:T(8,128)S(1)} fusion(bf16[512,4096]{1,0:T(8,128)(2,1)} %all-gather.2.cloned.1.call-done, bf16[4096,4096]{1,0:T(8,128)(2,1)} %get-tuple-element.361), kind=kOutput, calls=%fused_computation.14.clone.1 | convolution fusion | flops 17179869184 | bytes 46137344 | tf_op jit(solution)/shard_map/while/body/eval_jaxpr/dot_general | solution.py:39
  409.7 8.2 %copy.12 = f32[64,8,8,512]{3,2,1,0:T(8,128)S(1)} copy(f32[64,8,8,512]{3,1,2,0:T(8,128)S(1)} %bitcast.34) | data formatting | bytes 16777216 | tf_op jit(solution)/shard_map/while
  418.9 3.9 fusion.20
  424.9 3.4 collective-permute-start
  428.3 13.5 %collective-permute-done = bf16[512,512]{1,0:T(8,128)(2,1)S(1)} collective-permute-done((bf16[512,512]{1,0:T(8,128)(2,1)S(1)}, bf16[512,512]{1,0:T(8,128)(2,1)S(1)}, u32[]{:S(2)}, u32[]{:S(2)}) %collective-permute-start) | collective-permute-done | bytes 524320 | tf_op jit(solution)/shard_map/while/body/eval_jaxpr/ppermute | solution.py:12
  444.2 44.4 %all-gather.2.cloned.1.call-done = bf16[512,4096]{1,0:T(8,128)(2,1)} async-done(((bf16[512,512]{1,0:T(8,128)(2,1)}), bf16[512,4096]{1,0:T(8,128)(2,1)}) %all-gather.2.cloned.1.call-update) | async-done | bytes 4194320 | tf_op jit(solution)/shard_map/while/body/eval_jaxpr/all_gather | solution.py:38
  488.7 22.6 %fusion.18 = f32[512,4096]{1,0:T(8,128)S(1)} fusion(bf16[512,4096]{1,0:T(8,128)(2,1)} %all-gather.2.cloned.1.call-done, bf16[4096,4096]{1,0:T(8,128)(2,1)} %get-tuple-element.361), kind=kOutput, calls=%fused_computation.14.clone.1 | convolution fusion | flops 17179869184 | bytes 46137344 | tf_op jit(solution)/shard_map/while/body/eval_jaxpr/dot_general | solution.py:39
  511.3 8.2 %copy.12 = f32[64,8,8,512]{3,2,1,0:T(8,128)S(1)} copy(f32[64,8,8,512]{3,1,2,0:T(8,128)S(1)} %bitcast.34) | data formatting | bytes 16777216 | tf_op jit(solution)/shard_map/while
  520.6 3.9 fusion.20
  526.5 3.4 collective-permute-start
  529.9 13.5 %collective-permute-done = bf16[512,512]{1,0:T(8,128)(2,1)S(1)} collective-permute-done((bf16[512,512]{1,0:T(8,128)(2,1)S(1)}, bf16[512,512]{1,0:T(8,128)(2,1)S(1)}, u32[]{:S(2)}, u32[]{:S(2)}) %collective-permute-start) | collective-permute-done | bytes 524320 | tf_op jit(solution)/shard_map/while/body/eval_jaxpr/ppermute | solution.py:12
  (66 shorter events, 29.9 us)
Async XLA Ops:
  7.2 23.9 %copy-start.1 = (f32[1,8,8]{2,1,0:T(8,128)S(1)}, f32[1,8,8]{2,1,0:T(8,128)}, u32[]{:S(2)}) copy-start(f32[1,8,8]{2,1,0:T(8,128)} %param.10) | copy-start | bytes 772
  7.2 23.9 %copy-start.2 = (f32[1,8,4]{1,2,0:T(4,128)S(1)}, f32[1,8,4]{1,2,0:T(4,128)}, u32[]{:S(2)}) copy-start(f32[1,8,4]{1,2,0:T(4,128)} %param.9) | copy-start | bytes 388
  7.2 23.9 %copy-start.4 = (s32[1,1024]{1,0:T(1,128)S(1)}, s32[1,1024]{1,0:T(1,128)}, u32[]{:S(2)}) copy-start(s32[1,1024]{1,0:T(1,128)} %param.11) | copy-start | bytes 12292
  31.1 50.5 %all-gather.2.cloned.1.call-start = ((), (), s32[]{:S(2)}) async-start(), calls=%async_computation | async-start | bytes 4718592 | tf_op jit(solution)/shard_map/while/body/eval_jaxpr/all_gather | solution.py:38
  104.2 8.2 %copy-start = (bf16[512,4096]{1,0:T(8,128)(2,1)S(1)}, bf16[512,4096]{1,0:T(8,128)(2,1)}, u32[]{:S(2)}) copy-start(bf16[512,4096]{1,0:T(8,128)(2,1)} %all-gather.2.cloned.1.call-done) | copy-start | bytes 12582916 | tf_op jit(solution)/shard_map/while
  119.4 16.8 %collective-permute-start = (bf16[512,512]{1,0:T(8,128)(2,1)S(1)}, bf16[512,512]{1,0:T(8,128)(2,1)S(1)}, u32[]{:S(2)}, u32[]{:S(2)}) collective-permute-start(bf16[512,512]{1,0:T(8,128)(2,1)S(1)} %get-tuple-element.317), channel_id=1, source_target_pairs={{0,8},{8,16},{16,24},{1,9},{9,17},{17,25},{2,10},{10,18},{18,26},{... | collective-permute-start | bytes 1572872 | tf_op jit(solution)/shard_map/while/body/eval_jaxpr/ppermute | solution.py:12
  136.3 47.2 %all-gather.2.cloned.1.call-start = ((), (), s32[]{:S(2)}) async-start(), calls=%async_computation | async-start | bytes 4718592 | tf_op jit(solution)/shard_map/while/body/eval_jaxpr/all_gather | solution.py:38
  206.1 8.2 %copy-start = (bf16[512,4096]{1,0:T(8,128)(2,1)S(1)}, bf16[512,4096]{1,0:T(8,128)(2,1)}, u32[]{:S(2)}) copy-start(bf16[512,4096]{1,0:T(8,128)(2,1)} %all-gather.2.cloned.1.call-done) | copy-start | bytes 12582916 | tf_op jit(solution)/shard_map/while
  221.4 16.8 %collective-permute-start = (bf16[512,512]{1,0:T(8,128)(2,1)S(1)}, bf16[512,512]{1,0:T(8,128)(2,1)S(1)}, u32[]{:S(2)}, u32[]{:S(2)}) collective-permute-start(bf16[512,512]{1,0:T(8,128)(2,1)S(1)} %get-tuple-element.317), channel_id=1, source_target_pairs={{0,8},{8,16},{16,24},{1,9},{9,17},{17,25},{2,10},{10,18},{18,26},{... | collective-permute-start | bytes 1572872 | tf_op jit(solution)/shard_map/while/body/eval_jaxpr/ppermute | solution.py:12
  238.2 47.2 %all-gather.2.cloned.1.call-start = ((), (), s32[]{:S(2)}) async-start(), calls=%async_computation | async-start | bytes 4718592 | tf_op jit(solution)/shard_map/while/body/eval_jaxpr/all_gather | solution.py:38
  308.0 8.2 %copy-start = (bf16[512,4096]{1,0:T(8,128)(2,1)S(1)}, bf16[512,4096]{1,0:T(8,128)(2,1)}, u32[]{:S(2)}) copy-start(bf16[512,4096]{1,0:T(8,128)(2,1)} %all-gather.2.cloned.1.call-done) | copy-start | bytes 12582916 | tf_op jit(solution)/shard_map/while
  323.3 16.8 %collective-permute-start = (bf16[512,512]{1,0:T(8,128)(2,1)S(1)}, bf16[512,512]{1,0:T(8,128)(2,1)S(1)}, u32[]{:S(2)}, u32[]{:S(2)}) collective-permute-start(bf16[512,512]{1,0:T(8,128)(2,1)S(1)} %get-tuple-element.317), channel_id=1, source_target_pairs={{0,8},{8,16},{16,24},{1,9},{9,17},{17,25},{2,10},{10,18},{18,26},{... | collective-permute-start | bytes 1572872 | tf_op jit(solution)/shard_map/while/body/eval_jaxpr/ppermute | solution.py:12
  340.1 46.9 %all-gather.2.cloned.1.call-start = ((), (), s32[]{:S(2)}) async-start(), calls=%async_computation | async-start | bytes 4718592 | tf_op jit(solution)/shard_map/while/body/eval_jaxpr/all_gather | solution.py:38
  409.6 8.2 %copy-start = (bf16[512,4096]{1,0:T(8,128)(2,1)S(1)}, bf16[512,4096]{1,0:T(8,128)(2,1)}, u32[]{:S(2)}) copy-start(bf16[512,4096]{1,0:T(8,128)(2,1)} %all-gather.2.cloned.1.call-done) | copy-start | bytes 12582916 | tf_op jit(solution)/shard_map/while
  424.9 16.8 %collective-permute-start = (bf16[512,512]{1,0:T(8,128)(2,1)S(1)}, bf16[512,512]{1,0:T(8,128)(2,1)S(1)}, u32[]{:S(2)}, u32[]{:S(2)}) collective-permute-start(bf16[512,512]{1,0:T(8,128)(2,1)S(1)} %get-tuple-element.317), channel_id=1, source_target_pairs={{0,8},{8,16},{16,24},{1,9},{9,17},{17,25},{2,10},{10,18},{18,26},{... | collective-permute-start | bytes 1572872 | tf_op jit(solution)/shard_map/while/body/eval_jaxpr/ppermute | solution.py:12
  441.7 46.9 %all-gather.2.cloned.1.call-start = ((), (), s32[]{:S(2)}) async-start(), calls=%async_computation | async-start | bytes 4718592 | tf_op jit(solution)/shard_map/while/body/eval_jaxpr/all_gather | solution.py:38
  511.3 8.2 %copy-start = (bf16[512,4096]{1,0:T(8,128)(2,1)S(1)}, bf16[512,4096]{1,0:T(8,128)(2,1)}, u32[]{:S(2)}) copy-start(bf16[512,4096]{1,0:T(8,128)(2,1)} %all-gather.2.cloned.1.call-done) | copy-start | bytes 12582916 | tf_op jit(solution)/shard_map/while
  526.5 16.8 %collective-permute-start = (bf16[512,512]{1,0:T(8,128)(2,1)S(1)}, bf16[512,512]{1,0:T(8,128)(2,1)S(1)}, u32[]{:S(2)}, u32[]{:S(2)}) collective-permute-start(bf16[512,512]{1,0:T(8,128)(2,1)S(1)} %get-tuple-element.317), channel_id=1, source_target_pairs={{0,8},{8,16},{16,24},{1,9},{9,17},{17,25},{2,10},{10,18},{18,26},{... | collective-permute-start | bytes 1572872 | tf_op jit(solution)/shard_map/while/body/eval_jaxpr/ppermute | solution.py:12
  543.4 0.6 copy-start.3
Sparse Core Ops, SparseCore 0:
  33.5 48.0 all-gather.1
  138.7 44.7 all-gather.1
  240.6 44.7 all-gather.1
  342.2 44.7 all-gather.1
  443.9 44.7 all-gather.1
where the time goes:
time: 551 us
  waiting for transfers between devices  294 us (53%)
  matrix products  115 us (21%)
  local copies, waits for them, and re-layouts  66 us (12%)
  other arithmetic  45.2 us (8%)
  starting transfers between devices  16.9 us (3%)
  between operations  13.8 us (3%)
    all_gather x5, waiting for transfers between devices, tick(): piece = lax.all_gather(rows_in, 'bond', axis=1, tiled=True)  226 us
    dot_general x5, matrix products, tick(): total = jnp.dot(piece, a_mat, preferred_element_type=jnp.float32)  113 us
    ppermute x5, waiting for transfers between devices, shifted(): lax.ppermute(value, axis, [(source, source + steps) for source in range(i...  67.3 us
    while x15, local copies, waits for them, and re-layouts  40.9 us
    unnamed x9, local copies, waits for them, and re-layouts  23.3 us
    reduce_sum x5, other arithmetic, tick(): mixed = jnp.sum(weight[:, :, None] * prod, axis=1)  19.5 us
    ppermute x5, starting transfers between devices, shifted(): lax.ppermute(value, axis, [(source, source + steps) for source in range(i...  16.8 us
  transfers between devices with their start and end apart: 10, of which 10 were waited for; matrix products, arithmetic and copies ran while one was open for 0% of the time, Pallas kernels for 0%

commit v1 on v0

--- a/solution.py
+++ b/solution.py
@@ -4,6 +4,19 @@
 from jax.sharding import PartitionSpec as P
 
 ROWS = 512
+
+
+def gather_around(x, axis, dim):
+    ways = lax.axis_size(axis)
+    up = [(d, (d + 1) % ways) for d in range(ways)]
+    down = [(d, (d - 1) % ways) for d in range(ways)]
+    earlier, later = ([x], [x])
+    for _ in range(ways // 2):
+        earlier.append(lax.ppermute(earlier[-1], axis, up))
+    for _ in range((ways - 1) // 2):
+        later.append(lax.ppermute(later[-1], axis, down))
+    line = jnp.concatenate([*earlier[::-1], *later[1:]], axis=dim)
+    return jnp.roll(line, (lax.axis_index(axis) - ways // 2) * x.shape[dim], axis=dim)
 
 
 def shifted(value, axis, steps):
@@ -35,7 +48,7 @@
         first = jnp.clip(batch, 0, ngroups - 1) * grows
         start_piece = lax.dynamic_slice_in_dim(start_rows, first, grows, 0)
         rows_in = jnp.where(position == 0, start_piece, incoming)
-        piece = lax.all_gather(rows_in, "bond", axis=1, tiled=True)
+        piece = gather_around(rows_in, "bond", 1)
         total = jnp.dot(piece, a_mat, preferred_element_type=jnp.float32)
         pf = piece.astype(jnp.float32)
         total, squares = (total, jnp.sum(pf * pf, axis=1))

time: 551 us -> 531 us (0.964)
  waiting for transfers between devices: 294 us -> 239 us
  starting transfers between devices: 16.9 us -> 67.2 us
  local copies, waits for them, and re-layouts: 66 us -> 80.8 us
  other arithmetic: 45.2 us -> 32 us
  between operations: 13.8 us -> 0.67 us
    all_gather x5 -> x0, waiting for transfers between devices: 226 us -> none  [tick(): piece = lax.all_gather(rows_in, 'bond', axis=1, tiled=True)]
    ppermute x0 -> x35, waiting for transfers between devices: none -> 190 us  [the longest x20 179 us: gather_around(): earlier.append(lax.ppermute(earlier[-1], axis, up))]
    ppermute x0 -> x35, starting transfers between devices: none -> 55.5 us  [the longest x15 55.2 us: gather_around(): later.append(lax.ppermute(later[-1], axis, down))]
    ppermute x5, waiting for transfers between devices: 67.3 us -> 48.2 us  [shifted(): lax.ppermute(value, axis, [(source, source + steps) for source in range(i...]
    while x15 -> x100, local copies, waits for them, and re-layouts: 40.9 us -> 55.4 us
    select_n x5, other arithmetic: 10.4 us -> 1.24 us  [tick(): jnp.where(valid, lax.dynamic_update_slice_in_dim(out_leave, leave, first,...]
  transfers between devices with their start and end apart: 10 -> 40, of which waited for: 10 -> 34; matrix products, arithmetic and copies ran while one was open for 0% -> 2% of each run, Pallas kernels for 0% -> 0%
where the time goes in v1:
time: 531 us; the launch traced here: 530 us
  waiting for transfers between devices  239 us (45%)
  matrix products  110 us (21%)
  local copies, waits for them, and re-layouts  80.8 us (15%)
  starting transfers between devices  67.2 us (13%)
  other arithmetic  32 us (6%)
    ppermute x20, waiting for transfers between devices, gather_around(): earlier.append(lax.ppermute(earlier[-1], axis, up))  179 us
    dot_general x5, matrix products, tick(): total = jnp.dot(piece, a_mat, preferred_element_type=jnp.float32)  108 us
    while x100, local copies, waits for them, and re-layouts  55.4 us
    ppermute x15, starting transfers between devices, gather_around(): later.append(lax.ppermute(later[-1], axis, down))  55.2 us
    ppermute x5, waiting for transfers between devices, shifted(): lax.ppermute(value, axis, [(source, source + steps) for source in range(i...  48.2 us
    unnamed x9, local copies, waits for them, and re-layouts  23.3 us
    reduce_sum x5, other arithmetic, tick(): mixed = jnp.sum(weight[:, :, None] * prod, axis=1)  19.5 us
    ppermute x5, starting transfers between devices, shifted(): lax.ppermute(value, axis, [(source, source + steps) for source in range(i...  11.7 us
  transfers between devices with their start and end apart: 40, of which 34 were waited for; matrix products, arithmetic and copies ran while one was open for 2% of the time, Pallas kernels for 0%

profile of v1, /device:TPU:4, one launch (start us, length us, event | category | flops | bytes accessed | tf_op | source)
XLA Modules:
  0.0 530.2 jit_solution(11247330403048292650)
XLA Ops:
  0.7 22.7 %copy.10 = bf16[512,8,8,512]{3,1,2,0:T(8,128)(2,1)} copy(bf16[512,8,8,512]{3,2,1,0:T(8,128)(2,1)} %bitcast.32) | data formatting | bytes 67108864
  24.5 505.1 %while.19 = (s32[]{:T(128)}, bf16[512,512]{1,0:T(8,128)(2,1)S(1)}, bf16[1024,512]{1,0:T(8,128)(2,1)}, f32[1024]{0:T(1024)S(1)}, s32[]{:T(128)}, /*index=5*/s32[1...) while((s32[]{:T(128)}, bf16[512,512]{1,0:T(8,128)(2,1)S(1)}, ...), condition=%wide.region_3.4_spmd, body=%wide.region_0.3_spmd.sunk | while | flops 17193637888 | bytes 122768632 | solution.py:80
  25.8 10.4 %collective-permute-done = bf16[512,512]{1,0:T(8,128)(2,1)S(1)} collective-permute-done((bf16[512,512]{1,0:T(8,128)(2,1)S(1)}, bf16[512,512]{1,0:T(8,128)(2,1)S(1)}, u32[]{:S(2)}, u32[]{:S(2)}) %collective-permute-start) | collective-permute-done | bytes 524320 | tf_op jit(solution)/shard_map/while/body/eval_jaxpr/ppermute | solution.py:15
  39.7 12.2 %collective-permute-done.1 = bf16[512,512]{1,0:T(8,128)(2,1)S(1)} collective-permute-done((bf16[512,512]{1,0:T(8,128)(2,1)S(1)}, bf16[512,512]{1,0:T(8,128)(2,1)S(1)}, u32[]{:S(2)}, u32[]{:S(2)}) %collective-permute-start.1) | collective-permute-done | bytes 524320 | tf_op jit(solution)/shard_map/while/body/eval_jaxpr/ppermute | solution.py:15
  55.4 11.1 %collective-permute-done.2 = bf16[512,512]{1,0:T(8,128)(2,1)S(1)} collective-permute-done((bf16[512,512]{1,0:T(8,128)(2,1)S(1)}, bf16[512,512]{1,0:T(8,128)(2,1)S(1)}, u32[]{:S(2)}, u32[]{:S(2)}) %collective-permute-start.2) | collective-permute-done | bytes 524320 | tf_op jit(solution)/shard_map/while/body/eval_jaxpr/ppermute | solution.py:15
  71.4 8.3 %collective-permute-done.3 = bf16[512,512]{1,0:T(8,128)(2,1)} collective-permute-done((bf16[512,512]{1,0:T(8,128)(2,1)S(1)}, bf16[512,512]{1,0:T(8,128)(2,1)}, u32[]{:S(2)}, u32[]{:S(2)}) %collective-permute-start.3) | collective-permute-done | bytes 524320 | tf_op jit(solution)/shard_map/while/body/eval_jaxpr/ppermute | solution.py:15
  83.7 21.6 %fusion.19 = f32[512,4096]{1,0:T(8,128)S(1)} fusion(bf16[4096,4096]{1,0:T(8,128)(2,1)} %get-tuple-element.408, bf16[512,8192]{1,0:T(8,128)(2,1)S(1)} %constant_dynamic-update-slice_fusion.47, s32[]{:T(128)S(6)} %select_n.135), kind=kOutput, calls=%fused_computation.4.clone.1 | convolution fusion | flops 17179869184 | bytes 46137348 | tf_op jit(solution)/shard_map/while/body/eval_jaxpr/dot_general | solution.py:52
  105.3 8.1 %copy.12 = f32[64,8,8,512]{3,2,1,0:T(8,128)S(1)} copy(f32[64,8,8,512]{3,1,2,0:T(8,128)S(1)} %bitcast.31) | data formatting | bytes 16777216 | tf_op jit(solution)/shard_map/while
  121.2 8.6 %collective-permute-done.7 = bf16[512,512]{1,0:T(8,128)(2,1)S(1)} collective-permute-done((bf16[512,512]{1,0:T(8,128)(2,1)S(1)}, bf16[512,512]{1,0:T(8,128)(2,1)S(1)}, u32[]{:S(2)}, u32[]{:S(2)}) %collective-permute-start.7) | collective-permute-done | bytes 524320 | tf_op jit(solution)/shard_map/while/body/eval_jaxpr/ppermute | solution.py:25
  131.0 10.5 %collective-permute-done = bf16[512,512]{1,0:T(8,128)(2,1)S(1)} collective-permute-done((bf16[512,512]{1,0:T(8,128)(2,1)S(1)}, bf16[512,512]{1,0:T(8,128)(2,1)S(1)}, u32[]{:S(2)}, u32[]{:S(2)}) %collective-permute-start) | collective-permute-done | bytes 524320 | tf_op jit(solution)/shard_map/while/body/eval_jaxpr/ppermute | solution.py:15
  145.1 8.9 %collective-permute-done.1 = bf16[512,512]{1,0:T(8,128)(2,1)S(1)} collective-permute-done((bf16[512,512]{1,0:T(8,128)(2,1)S(1)}, bf16[512,512]{1,0:T(8,128)(2,1)S(1)}, u32[]{:S(2)}, u32[]{:S(2)}) %collective-permute-start.1) | collective-permute-done | bytes 524320 | tf_op jit(solution)/shard_map/while/body/eval_jaxpr/ppermute | solution.py:15
  171.4 8.2 %collective-permute-done.3 = bf16[512,512]{1,0:T(8,128)(2,1)} collective-permute-done((bf16[512,512]{1,0:T(8,128)(2,1)S(1)}, bf16[512,512]{1,0:T(8,128)(2,1)}, u32[]{:S(2)}, u32[]{:S(2)}) %collective-permute-start.3) | collective-permute-done | bytes 524320 | tf_op jit(solution)/shard_map/while/body/eval_jaxpr/ppermute | solution.py:15
  183.6 21.6 %fusion.19 = f32[512,4096]{1,0:T(8,128)S(1)} fusion(bf16[4096,4096]{1,0:T(8,128)(2,1)} %get-tuple-element.408, bf16[512,8192]{1,0:T(8,128)(2,1)S(1)} %constant_dynamic-update-slice_fusion.47, s32[]{:T(128)S(6)} %select_n.135), kind=kOutput, calls=%fused_computation.4.clone.1 | convolution fusion | flops 17179869184 | bytes 46137348 | tf_op jit(solution)/shard_map/while/body/eval_jaxpr/dot_general | solution.py:52
  205.2 8.1 %copy.12 = f32[64,8,8,512]{3,2,1,0:T(8,128)S(1)} copy(f32[64,8,8,512]{3,1,2,0:T(8,128)S(1)} %bitcast.31) | data formatting | bytes 16777216 | tf_op jit(solution)/shard_map/while
  220.2 9.5 %collective-permute-done.7 = bf16[512,512]{1,0:T(8,128)(2,1)S(1)} collective-permute-done((bf16[512,512]{1,0:T(8,128)(2,1)S(1)}, bf16[512,512]{1,0:T(8,128)(2,1)S(1)}, u32[]{:S(2)}, u32[]{:S(2)}) %collective-permute-start.7) | collective-permute-done | bytes 524320 | tf_op jit(solution)/shard_map/while/body/eval_jaxpr/ppermute | solution.py:25
  230.9 10.5 %collective-permute-done = bf16[512,512]{1,0:T(8,128)(2,1)S(1)} collective-permute-done((bf16[512,512]{1,0:T(8,128)(2,1)S(1)}, bf16[512,512]{1,0:T(8,128)(2,1)S(1)}, u32[]{:S(2)}, u32[]{:S(2)}) %collective-permute-start) | collective-permute-done | bytes 524320 | tf_op jit(solution)/shard_map/while/body/eval_jaxpr/ppermute | solution.py:15
  245.0 8.9 %collective-permute-done.1 = bf16[512,512]{1,0:T(8,128)(2,1)S(1)} collective-permute-done((bf16[512,512]{1,0:T(8,128)(2,1)S(1)}, bf16[512,512]{1,0:T(8,128)(2,1)S(1)}, u32[]{:S(2)}, u32[]{:S(2)}) %collective-permute-start.1) | collective-permute-done | bytes 524320 | tf_op jit(solution)/shard_map/while/body/eval_jaxpr/ppermute | solution.py:15
  283.5 21.6 %fusion.19 = f32[512,4096]{1,0:T(8,128)S(1)} fusion(bf16[4096,4096]{1,0:T(8,128)(2,1)} %get-tuple-element.408, bf16[512,8192]{1,0:T(8,128)(2,1)S(1)} %constant_dynamic-update-slice_fusion.47, s32[]{:T(128)S(6)} %select_n.135), kind=kOutput, calls=%fused_computation.4.clone.1 | convolution fusion | flops 17179869184 | bytes 46137348 | tf_op jit(solution)/shard_map/while/body/eval_jaxpr/dot_general | solution.py:52
  305.1 8.1 %copy.12 = f32[64,8,8,512]{3,2,1,0:T(8,128)S(1)} copy(f32[64,8,8,512]{3,1,2,0:T(8,128)S(1)} %bitcast.31) | data formatting | bytes 16777216 | tf_op jit(solution)/shard_map/while
  319.5 10.0 %collective-permute-done.7 = bf16[512,512]{1,0:T(8,128)(2,1)S(1)} collective-permute-done((bf16[512,512]{1,0:T(8,128)(2,1)S(1)}, bf16[512,512]{1,0:T(8,128)(2,1)S(1)}, u32[]{:S(2)}, u32[]{:S(2)}) %collective-permute-start.7) | collective-permute-done | bytes 524320 | tf_op jit(solution)/shard_map/while/body/eval_jaxpr/ppermute | solution.py:25
  330.8 10.5 %collective-permute-done = bf16[512,512]{1,0:T(8,128)(2,1)S(1)} collective-permute-done((bf16[512,512]{1,0:T(8,128)(2,1)S(1)}, bf16[512,512]{1,0:T(8,128)(2,1)S(1)}, u32[]{:S(2)}, u32[]{:S(2)}) %collective-permute-start) | collective-permute-done | bytes 524320 | tf_op jit(solution)/shard_map/while/body/eval_jaxpr/ppermute | solution.py:15
  344.9 9.0 %collective-permute-done.1 = bf16[512,512]{1,0:T(8,128)(2,1)S(1)} collective-permute-done((bf16[512,512]{1,0:T(8,128)(2,1)S(1)}, bf16[512,512]{1,0:T(8,128)(2,1)S(1)}, u32[]{:S(2)}, u32[]{:S(2)}) %collective-permute-start.1) | collective-permute-done | bytes 524320 | tf_op jit(solution)/shard_map/while/body/eval_jaxpr/ppermute | solution.py:15
  371.2 8.2 %collective-permute-done.3 = bf16[512,512]{1,0:T(8,128)(2,1)} collective-permute-done((bf16[512,512]{1,0:T(8,128)(2,1)S(1)}, bf16[512,512]{1,0:T(8,128)(2,1)}, u32[]{:S(2)}, u32[]{:S(2)}) %collective-permute-start.3) | collective-permute-done | bytes 524320 | tf_op jit(solution)/shard_map/while/body/eval_jaxpr/ppermute | solution.py:15
  383.5 21.6 %fusion.19 = f32[512,4096]{1,0:T(8,128)S(1)} fusion(bf16[4096,4096]{1,0:T(8,128)(2,1)} %get-tuple-element.408, bf16[512,8192]{1,0:T(8,128)(2,1)S(1)} %constant_dynamic-update-slice_fusion.47, s32[]{:T(128)S(6)} %select_n.135), kind=kOutput, calls=%fused_computation.4.clone.1 | convolution fusion | flops 17179869184 | bytes 46137348 | tf_op jit(solution)/shard_map/while/body/eval_jaxpr/dot_general | solution.py:52
  405.1 8.1 %copy.12 = f32[64,8,8,512]{3,2,1,0:T(8,128)S(1)} copy(f32[64,8,8,512]{3,1,2,0:T(8,128)S(1)} %bitcast.31) | data formatting | bytes 16777216 | tf_op jit(solution)/shard_map/while
  419.5 10.0 %collective-permute-done.7 = bf16[512,512]{1,0:T(8,128)(2,1)S(1)} collective-permute-done((bf16[512,512]{1,0:T(8,128)(2,1)S(1)}, bf16[512,512]{1,0:T(8,128)(2,1)S(1)}, u32[]{:S(2)}, u32[]{:S(2)}) %collective-permute-start.7) | collective-permute-done | bytes 524320 | tf_op jit(solution)/shard_map/while/body/eval_jaxpr/ppermute | solution.py:25
  430.8 10.5 %collective-permute-done = bf16[512,512]{1,0:T(8,128)(2,1)S(1)} collective-permute-done((bf16[512,512]{1,0:T(8,128)(2,1)S(1)}, bf16[512,512]{1,0:T(8,128)(2,1)S(1)}, u32[]{:S(2)}, u32[]{:S(2)}) %collective-permute-start) | collective-permute-done | bytes 524320 | tf_op jit(solution)/shard_map/while/body/eval_jaxpr/ppermute | solution.py:15
  444.8 9.0 %collective-permute-done.1 = bf16[512,512]{1,0:T(8,128)(2,1)S(1)} collective-permute-done((bf16[512,512]{1,0:T(8,128)(2,1)S(1)}, bf16[512,512]{1,0:T(8,128)(2,1)S(1)}, u32[]{:S(2)}, u32[]{:S(2)}) %collective-permute-start.1) | collective-permute-done | bytes 524320 | tf_op jit(solution)/shard_map/while/body/eval_jaxpr/ppermute | solution.py:15
  471.2 8.2 %collective-permute-done.3 = bf16[512,512]{1,0:T(8,128)(2,1)} collective-permute-done((bf16[512,512]{1,0:T(8,128)(2,1)S(1)}, bf16[512,512]{1,0:T(8,128)(2,1)}, u32[]{:S(2)}, u32[]{:S(2)}) %collective-permute-start.3) | collective-permute-done | bytes 524320 | tf_op jit(solution)/shard_map/while/body/eval_jaxpr/ppermute | solution.py:15
  483.5 21.6 %fusion.19 = f32[512,4096]{1,0:T(8,128)S(1)} fusion(bf16[4096,4096]{1,0:T(8,128)(2,1)} %get-tuple-element.408, bf16[512,8192]{1,0:T(8,128)(2,1)S(1)} %constant_dynamic-update-slice_fusion.47, s32[]{:T(128)S(6)} %select_n.135), kind=kOutput, calls=%fused_computation.4.clone.1 | convolution fusion | flops 17179869184 | bytes 46137348 | tf_op jit(solution)/shard_map/while/body/eval_jaxpr/dot_general | solution.py:52
  505.1 8.1 %copy.12 = f32[64,8,8,512]{3,2,1,0:T(8,128)S(1)} copy(f32[64,8,8,512]{3,1,2,0:T(8,128)S(1)} %bitcast.31) | data formatting | bytes 16777216 | tf_op jit(solution)/shard_map/while
  519.5 10.0 %collective-permute-done.7 = bf16[512,512]{1,0:T(8,128)(2,1)S(1)} collective-permute-done((bf16[512,512]{1,0:T(8,128)(2,1)S(1)}, bf16[512,512]{1,0:T(8,128)(2,1)S(1)}, u32[]{:S(2)}, u32[]{:S(2)}) %collective-permute-start.7) | collective-permute-done | bytes 524320 | tf_op jit(solution)/shard_map/while/body/eval_jaxpr/ppermute | solution.py:25
  (211 shorter events, 164.5 us)
Async XLA Ops:
  36.2 15.7 %collective-permute-start.1 = (bf16[512,512]{1,0:T(8,128)(2,1)S(1)}, bf16[512,512]{1,0:T(8,128)(2,1)S(1)}, u32[]{:S(2)}, u32[]{:S(2)}) collective-permute-start(bf16[512,512]{1,0:T(8,128)(2,1)S(1)} %collective-permute-done), channel_id=1, source_target_pairs={{0,1},{1,2},{2,3},{3,4},{4,5},{5,6},{6,7},{7,0},{8,9},{9,10},{10,1... | collective-permute-start | bytes 1572872 | tf_op jit(solution)/shard_map/while/body/eval_jaxpr/ppermute | solution.py:15
  36.2 15.7 %collective-permute-start.4 = (bf16[512,512]{1,0:T(8,128)(2,1)S(1)}, bf16[512,512]{1,0:T(8,128)(2,1)S(1)}, u32[]{:S(2)}, u32[]{:S(2)}) collective-permute-start(bf16[512,512]{1,0:T(8,128)(2,1)S(1)} %dynamic-slice_select_fusion.2), channel_id=1, source_target_pairs={{0,7},{1,0},{2,1},{3,2},{4,3},{5,4},{6,5},{7,6},{8,15},{9,8},{10,9... | collective-permute-start | bytes 1572872 | tf_op jit(solution)/shard_map/while/body/eval_jaxpr/ppermute | solution.py:17
  51.9 14.6 %collective-permute-start.2 = (bf16[512,512]{1,0:T(8,128)(2,1)S(1)}, bf16[512,512]{1,0:T(8,128)(2,1)S(1)}, u32[]{:S(2)}, u32[]{:S(2)}) collective-permute-start(bf16[512,512]{1,0:T(8,128)(2,1)S(1)} %collective-permute-done.1), channel_id=1, source_target_pairs={{0,1},{1,2},{2,3},{3,4},{4,5},{5,6},{6,7},{7,0},{8,9},{9,10},{10,1... | collective-permute-start | bytes 1572872 | tf_op jit(solution)/shard_map/while/body/eval_jaxpr/ppermute | solution.py:15
  51.9 15.7 %collective-permute-start.5 = (bf16[512,512]{1,0:T(8,128)(2,1)S(1)}, bf16[512,512]{1,0:T(8,128)(2,1)S(1)}, u32[]{:S(2)}, u32[]{:S(2)}) collective-permute-start(bf16[512,512]{1,0:T(8,128)(2,1)S(1)} %collective-permute-done.4), channel_id=1, source_target_pairs={{0,7},{1,0},{2,1},{3,2},{4,3},{5,4},{6,5},{7,6},{8,15},{9,8},{10,9... | collective-permute-start | bytes 1572872 | tf_op jit(solution)/shard_map/while/body/eval_jaxpr/ppermute | solution.py:17
  66.5 13.1 %collective-permute-start.3 = (bf16[512,512]{1,0:T(8,128)(2,1)S(1)}, bf16[512,512]{1,0:T(8,128)(2,1)}, u32[]{:S(2)}, u32[]{:S(2)}) collective-permute-start(bf16[512,512]{1,0:T(8,128)(2,1)S(1)} %collective-permute-done.2), channel_id=1, source_target_pairs={{0,1},{1,2},{2,3},{3,4},{4,5},{5,6},{6,7},{7,0},{8,9},{9,10},{10,1... | collective-permute-start | bytes 1572872 | tf_op jit(solution)/shard_map/while/body/eval_jaxpr/ppermute | solution.py:15
  67.6 13.6 %collective-permute-start.6 = (bf16[512,512]{1,0:T(8,128)(2,1)S(1)}, bf16[512,512]{1,0:T(8,128)(2,1)S(1)}, u32[]{:S(2)}, u32[]{:S(2)}) collective-permute-start(bf16[512,512]{1,0:T(8,128)(2,1)S(1)} %collective-permute-done.5), channel_id=1, source_target_pairs={{0,7},{1,0},{2,1},{3,2},{4,3},{5,4},{6,5},{7,6},{8,15},{9,8},{10,9... | collective-permute-start | bytes 1572872 | tf_op jit(solution)/shard_map/while/body/eval_jaxpr/ppermute | solution.py:17
  117.8 12.0 %collective-permute-start.7 = (bf16[512,512]{1,0:T(8,128)(2,1)S(1)}, bf16[512,512]{1,0:T(8,128)(2,1)S(1)}, u32[]{:S(2)}, u32[]{:S(2)}) collective-permute-start(bf16[512,512]{1,0:T(8,128)(2,1)S(1)} %get-tuple-element.354), channel_id=1, source_target_pairs={{0,8},{8,16},{16,24},{1,9},{9,17},{17,25},{2,10},{10,18},{18,26},{... | collective-permute-start | bytes 1572872 | tf_op jit(solution)/shard_map/while/body/eval_jaxpr/ppermute | solution.py:25
  141.5 12.5 %collective-permute-start.1 = (bf16[512,512]{1,0:T(8,128)(2,1)S(1)}, bf16[512,512]{1,0:T(8,128)(2,1)S(1)}, u32[]{:S(2)}, u32[]{:S(2)}) collective-permute-start(bf16[512,512]{1,0:T(8,128)(2,1)S(1)} %collective-permute-done), channel_id=1, source_target_pairs={{0,1},{1,2},{2,3},{3,4},{4,5},{5,6},{6,7},{7,0},{8,9},{9,10},{10,1... | collective-permute-start | bytes 1572872 | tf_op jit(solution)/shard_map/while/body/eval_jaxpr/ppermute | solution.py:15
  141.5 13.5 %collective-permute-start.4 = (bf16[512,512]{1,0:T(8,128)(2,1)S(1)}, bf16[512,512]{1,0:T(8,128)(2,1)S(1)}, u32[]{:S(2)}, u32[]{:S(2)}) collective-permute-start(bf16[512,512]{1,0:T(8,128)(2,1)S(1)} %dynamic-slice_select_fusion.2), channel_id=1, source_target_pairs={{0,7},{1,0},{2,1},{3,2},{4,3},{5,4},{6,5},{7,6},{8,15},{9,8},{10,9... | collective-permute-start | bytes 1572872 | tf_op jit(solution)/shard_map/while/body/eval_jaxpr/ppermute | solution.py:17
  154.0 12.5 %collective-permute-start.2 = (bf16[512,512]{1,0:T(8,128)(2,1)S(1)}, bf16[512,512]{1,0:T(8,128)(2,1)S(1)}, u32[]{:S(2)}, u32[]{:S(2)}) collective-permute-start(bf16[512,512]{1,0:T(8,128)(2,1)S(1)} %collective-permute-done.1), channel_id=1, source_target_pairs={{0,1},{1,2},{2,3},{3,4},{4,5},{5,6},{6,7},{7,0},{8,9},{9,10},{10,1... | collective-permute-start | bytes 1572872 | tf_op jit(solution)/shard_map/while/body/eval_jaxpr/ppermute | solution.py:15
  155.1 12.5 %collective-permute-start.5 = (bf16[512,512]{1,0:T(8,128)(2,1)S(1)}, bf16[512,512]{1,0:T(8,128)(2,1)S(1)}, u32[]{:S(2)}, u32[]{:S(2)}) collective-permute-start(bf16[512,512]{1,0:T(8,128)(2,1)S(1)} %collective-permute-done.4), channel_id=1, source_target_pairs={{0,7},{1,0},{2,1},{3,2},{4,3},{5,4},{6,5},{7,6},{8,15},{9,8},{10,9... | collective-permute-start | bytes 1572872 | tf_op jit(solution)/shard_map/while/body/eval_jaxpr/ppermute | solution.py:17
  166.5 13.0 %collective-permute-start.3 = (bf16[512,512]{1,0:T(8,128)(2,1)S(1)}, bf16[512,512]{1,0:T(8,128)(2,1)}, u32[]{:S(2)}, u32[]{:S(2)}) collective-permute-start(bf16[512,512]{1,0:T(8,128)(2,1)S(1)} %collective-permute-done.2), channel_id=1, source_target_pairs={{0,1},{1,2},{2,3},{3,4},{4,5},{5,6},{6,7},{7,0},{8,9},{9,10},{10,1... | collective-permute-start | bytes 1572872 | tf_op jit(solution)/shard_map/while/body/eval_jaxpr/ppermute | solution.py:15
  167.6 13.5 %collective-permute-start.6 = (bf16[512,512]{1,0:T(8,128)(2,1)S(1)}, bf16[512,512]{1,0:T(8,128)(2,1)S(1)}, u32[]{:S(2)}, u32[]{:S(2)}) collective-permute-start(bf16[512,512]{1,0:T(8,128)(2,1)S(1)} %collective-permute-done.5), channel_id=1, source_target_pairs={{0,7},{1,0},{2,1},{3,2},{4,3},{5,4},{6,5},{7,6},{8,15},{9,8},{10,9... | collective-permute-start | bytes 1572872 | tf_op jit(solution)/shard_map/while/body/eval_jaxpr/ppermute | solution.py:17
  217.7 12.0 %collective-permute-start.7 = (bf16[512,512]{1,0:T(8,128)(2,1)S(1)}, bf16[512,512]{1,0:T(8,128)(2,1)S(1)}, u32[]{:S(2)}, u32[]{:S(2)}) collective-permute-start(bf16[512,512]{1,0:T(8,128)(2,1)S(1)} %get-tuple-element.354), channel_id=1, source_target_pairs={{0,8},{8,16},{16,24},{1,9},{9,17},{17,25},{2,10},{10,18},{18,26},{... | collective-permute-start | bytes 1572872 | tf_op jit(solution)/shard_map/while/body/eval_jaxpr/ppermute | solution.py:25
  241.5 12.4 %collective-permute-start.1 = (bf16[512,512]{1,0:T(8,128)(2,1)S(1)}, bf16[512,512]{1,0:T(8,128)(2,1)S(1)}, u32[]{:S(2)}, u32[]{:S(2)}) collective-permute-start(bf16[512,512]{1,0:T(8,128)(2,1)S(1)} %collective-permute-done), channel_id=1, source_target_pairs={{0,1},{1,2},{2,3},{3,4},{4,5},{5,6},{6,7},{7,0},{8,9},{9,10},{10,1... | collective-permute-start | bytes 1572872 | tf_op jit(solution)/shard_map/while/body/eval_jaxpr/ppermute | solution.py:15
  241.5 15.1 %collective-permute-start.4 = (bf16[512,512]{1,0:T(8,128)(2,1)S(1)}, bf16[512,512]{1,0:T(8,128)(2,1)S(1)}, u32[]{:S(2)}, u32[]{:S(2)}) collective-permute-start(bf16[512,512]{1,0:T(8,128)(2,1)S(1)} %dynamic-slice_select_fusion.2), channel_id=1, source_target_pairs={{0,7},{1,0},{2,1},{3,2},{4,3},{5,4},{6,5},{7,6},{8,15},{9,8},{10,9... | collective-permute-start | bytes 1572872 | tf_op jit(solution)/shard_map/while/body/eval_jaxpr/ppermute | solution.py:17
  253.9 12.5 %collective-permute-start.2 = (bf16[512,512]{1,0:T(8,128)(2,1)S(1)}, bf16[512,512]{1,0:T(8,128)(2,1)S(1)}, u32[]{:S(2)}, u32[]{:S(2)}) collective-permute-start(bf16[512,512]{1,0:T(8,128)(2,1)S(1)} %collective-permute-done.1), channel_id=1, source_target_pairs={{0,1},{1,2},{2,3},{3,4},{4,5},{5,6},{6,7},{7,0},{8,9},{9,10},{10,1... | collective-permute-start | bytes 1572872 | tf_op jit(solution)/shard_map/while/body/eval_jaxpr/ppermute | solution.py:15
  256.6 13.5 %collective-permute-start.5 = (bf16[512,512]{1,0:T(8,128)(2,1)S(1)}, bf16[512,512]{1,0:T(8,128)(2,1)S(1)}, u32[]{:S(2)}, u32[]{:S(2)}) collective-permute-start(bf16[512,512]{1,0:T(8,128)(2,1)S(1)} %collective-permute-done.4), channel_id=1, source_target_pairs={{0,7},{1,0},{2,1},{3,2},{4,3},{5,4},{6,5},{7,6},{8,15},{9,8},{10,9... | collective-permute-start | bytes 1572872 | tf_op jit(solution)/shard_map/while/body/eval_jaxpr/ppermute | solution.py:17
  266.4 13.0 %collective-permute-start.3 = (bf16[512,512]{1,0:T(8,128)(2,1)S(1)}, bf16[512,512]{1,0:T(8,128)(2,1)}, u32[]{:S(2)}, u32[]{:S(2)}) collective-permute-start(bf16[512,512]{1,0:T(8,128)(2,1)S(1)} %collective-permute-done.2), channel_id=1, source_target_pairs={{0,1},{1,2},{2,3},{3,4},{4,5},{5,6},{6,7},{7,0},{8,9},{9,10},{10,1... | collective-permute-start | bytes 1572872 | tf_op jit(solution)/shard_map/while/body/eval_jaxpr/ppermute | solution.py:15
  341.3 12.5 %collective-permute-start.1 = (bf16[512,512]{1,0:T(8,128)(2,1)S(1)}, bf16[512,512]{1,0:T(8,128)(2,1)S(1)}, u32[]{:S(2)}, u32[]{:S(2)}) collective-permute-start(bf16[512,512]{1,0:T(8,128)(2,1)S(1)} %collective-permute-done), channel_id=1, source_target_pairs={{0,1},{1,2},{2,3},{3,4},{4,5},{5,6},{6,7},{7,0},{8,9},{9,10},{10,1... | collective-permute-start | bytes 1572872 | tf_op jit(solution)/shard_map/while/body/eval_jaxpr/ppermute | solution.py:15
  341.3 13.6 %collective-permute-start.4 = (bf16[512,512]{1,0:T(8,128)(2,1)S(1)}, bf16[512,512]{1,0:T(8,128)(2,1)S(1)}, u32[]{:S(2)}, u32[]{:S(2)}) collective-permute-start(bf16[512,512]{1,0:T(8,128)(2,1)S(1)} %dynamic-slice_select_fusion.2), channel_id=1, source_target_pairs={{0,7},{1,0},{2,1},{3,2},{4,3},{5,4},{6,5},{7,6},{8,15},{9,8},{10,9... | collective-permute-start | bytes 1572872 | tf_op jit(solution)/shard_map/while/body/eval_jaxpr/ppermute | solution.py:17
  353.9 12.5 %collective-permute-start.2 = (bf16[512,512]{1,0:T(8,128)(2,1)S(1)}, bf16[512,512]{1,0:T(8,128)(2,1)S(1)}, u32[]{:S(2)}, u32[]{:S(2)}) collective-permute-start(bf16[512,512]{1,0:T(8,128)(2,1)S(1)} %collective-permute-done.1), channel_id=1, source_target_pairs={{0,1},{1,2},{2,3},{3,4},{4,5},{5,6},{6,7},{7,0},{8,9},{9,10},{10,1... | collective-permute-start | bytes 1572872 | tf_op jit(solution)/shard_map/while/body/eval_jaxpr/ppermute | solution.py:15
  354.9 12.5 %collective-permute-start.5 = (bf16[512,512]{1,0:T(8,128)(2,1)S(1)}, bf16[512,512]{1,0:T(8,128)(2,1)S(1)}, u32[]{:S(2)}, u32[]{:S(2)}) collective-permute-start(bf16[512,512]{1,0:T(8,128)(2,1)S(1)} %collective-permute-done.4), channel_id=1, source_target_pairs={{0,7},{1,0},{2,1},{3,2},{4,3},{5,4},{6,5},{7,6},{8,15},{9,8},{10,9... | collective-permute-start | bytes 1572872 | tf_op jit(solution)/shard_map/while/body/eval_jaxpr/ppermute | solution.py:17
  366.4 13.1 %collective-permute-start.3 = (bf16[512,512]{1,0:T(8,128)(2,1)S(1)}, bf16[512,512]{1,0:T(8,128)(2,1)}, u32[]{:S(2)}, u32[]{:S(2)}) collective-permute-start(bf16[512,512]{1,0:T(8,128)(2,1)S(1)} %collective-permute-done.2), channel_id=1, source_target_pairs={{0,1},{1,2},{2,3},{3,4},{4,5},{5,6},{6,7},{7,0},{8,9},{9,10},{10,1... | collective-permute-start | bytes 1572872 | tf_op jit(solution)/shard_map/while/body/eval_jaxpr/ppermute | solution.py:15
  367.4 13.5 %collective-permute-start.6 = (bf16[512,512]{1,0:T(8,128)(2,1)S(1)}, bf16[512,512]{1,0:T(8,128)(2,1)S(1)}, u32[]{:S(2)}, u32[]{:S(2)}) collective-permute-start(bf16[512,512]{1,0:T(8,128)(2,1)S(1)} %collective-permute-done.5), channel_id=1, source_target_pairs={{0,7},{1,0},{2,1},{3,2},{4,3},{5,4},{6,5},{7,6},{8,15},{9,8},{10,9... | collective-permute-start | bytes 1572872 | tf_op jit(solution)/shard_map/while/body/eval_jaxpr/ppermute | solution.py:17
  441.3 12.6 %collective-permute-start.1 = (bf16[512,512]{1,0:T(8,128)(2,1)S(1)}, bf16[512,512]{1,0:T(8,128)(2,1)S(1)}, u32[]{:S(2)}, u32[]{:S(2)}) collective-permute-start(bf16[512,512]{1,0:T(8,128)(2,1)S(1)} %collective-permute-done), channel_id=1, source_target_pairs={{0,1},{1,2},{2,3},{3,4},{4,5},{5,6},{6,7},{7,0},{8,9},{9,10},{10,1... | collective-permute-start | bytes 1572872 | tf_op jit(solution)/shard_map/while/body/eval_jaxpr/ppermute | solution.py:15
  441.3 13.6 %collective-permute-start.4 = (bf16[512,512]{1,0:T(8,128)(2,1)S(1)}, bf16[512,512]{1,0:T(8,128)(2,1)S(1)}, u32[]{:S(2)}, u32[]{:S(2)}) collective-permute-start(bf16[512,512]{1,0:T(8,128)(2,1)S(1)} %dynamic-slice_select_fusion.2), channel_id=1, source_target_pairs={{0,7},{1,0},{2,1},{3,2},{4,3},{5,4},{6,5},{7,6},{8,15},{9,8},{10,9... | collective-permute-start | bytes 1572872 | tf_op jit(solution)/shard_map/while/body/eval_jaxpr/ppermute | solution.py:17
  453.9 12.5 %collective-permute-start.2 = (bf16[512,512]{1,0:T(8,128)(2,1)S(1)}, bf16[512,512]{1,0:T(8,128)(2,1)S(1)}, u32[]{:S(2)}, u32[]{:S(2)}) collective-permute-start(bf16[512,512]{1,0:T(8,128)(2,1)S(1)} %collective-permute-done.1), channel_id=1, source_target_pairs={{0,1},{1,2},{2,3},{3,4},{4,5},{5,6},{6,7},{7,0},{8,9},{9,10},{10,1... | collective-permute-start | bytes 1572872 | tf_op jit(solution)/shard_map/while/body/eval_jaxpr/ppermute | solution.py:15
  454.9 12.6 %collective-permute-start.5 = (bf16[512,512]{1,0:T(8,128)(2,1)S(1)}, bf16[512,512]{1,0:T(8,128)(2,1)S(1)}, u32[]{:S(2)}, u32[]{:S(2)}) collective-permute-start(bf16[512,512]{1,0:T(8,128)(2,1)S(1)} %collective-permute-done.4), channel_id=1, source_target_pairs={{0,7},{1,0},{2,1},{3,2},{4,3},{5,4},{6,5},{7,6},{8,15},{9,8},{10,9... | collective-permute-start | bytes 1572872 | tf_op jit(solution)/shard_map/while/body/eval_jaxpr/ppermute | solution.py:17
  466.4 13.1 %collective-permute-start.3 = (bf16[512,512]{1,0:T(8,128)(2,1)S(1)}, bf16[512,512]{1,0:T(8,128)(2,1)}, u32[]{:S(2)}, u32[]{:S(2)}) collective-permute-start(bf16[512,512]{1,0:T(8,128)(2,1)S(1)} %collective-permute-done.2), channel_id=1, source_target_pairs={{0,1},{1,2},{2,3},{3,4},{4,5},{5,6},{6,7},{7,0},{8,9},{9,10},{10,1... | collective-permute-start | bytes 1572872 | tf_op jit(solution)/shard_map/while/body/eval_jaxpr/ppermute | solution.py:15
  467.5 13.5 %collective-permute-start.6 = (bf16[512,512]{1,0:T(8,128)(2,1)S(1)}, bf16[512,512]{1,0:T(8,128)(2,1)S(1)}, u32[]{:S(2)}, u32[]{:S(2)}) collective-permute-start(bf16[512,512]{1,0:T(8,128)(2,1)S(1)} %collective-permute-done.5), channel_id=1, source_target_pairs={{0,7},{1,0},{2,1},{3,2},{4,3},{5,4},{6,5},{7,6},{8,15},{9,8},{10,9... | collective-permute-start | bytes 1572872 | tf_op jit(solution)/shard_map/while/body/eval_jaxpr/ppermute | solution.py:17
  517.6 12.0 %collective-permute-start.7 = (bf16[512,512]{1,0:T(8,128)(2,1)S(1)}, bf16[512,512]{1,0:T(8,128)(2,1)S(1)}, u32[]{:S(2)}, u32[]{:S(2)}) collective-permute-start(bf16[512,512]{1,0:T(8,128)(2,1)S(1)} %get-tuple-element.354), channel_id=1, source_target_pairs={{0,8},{8,16},{16,24},{1,9},{9,17},{17,25},{2,10},{10,18},{18,26},{... | collective-permute-start | bytes 1572872 | tf_op jit(solution)/shard_map/while/body/eval_jaxpr/ppermute | solution.py:25
  (22 other events, 240.1 us)
